TPU v7x, 32 devices: a whole 2x2x4 slice. The times are simulated.
32 devices in a mesh: replica: 2 (over y), ctx: 4 (over z), head: 2 (over x), sub: 2 (over core).
Axes of the slice: x: 2, y: 2, z: 4, core: 2. Of those that a mesh axis runs over, the one named last changes fastest.
Arguments:
- queries: bfloat16 [8192, 2048], P(('replica', 'ctx', 'sub'), 'head'), parts along dimension 0, may hold values from -64 to 64
- keys: bfloat16 [8192, 1024], P(('replica', 'ctx', 'sub'), 'head'), parts along dimension 0, may hold values from -16 to 16
- values: bfloat16 [8192, 1024], P(('replica', 'ctx', 'sub'), 'head'), parts along dimension 0, may hold values from -6 to 6
- segment: int32 [8192], P(('replica', 'ctx', 'sub')), parts along dimension 0, may hold values from 0 to 1, as said below
- cotangent: bfloat16 [8192, 2560], P(('replica', 'ctx', 'sub')), parts along dimension 0, may hold values from -96 to 96
- out_weight: bfloat16 [2560, 2048], P(None, 'head'), may hold values from -0.125 to 0.125
Outputs:
- grad_queries: bfloat16 [8192, 2048], P(('replica', 'ctx', 'sub'), 'head'), parts along dimension 0
- grad_keys: bfloat16 [8192, 1024], P(('replica', 'ctx', 'sub'), 'head'), parts along dimension 0
- grad_values: bfloat16 [8192, 1024], P(('replica', 'ctx', 'sub'), 'head'), parts along dimension 0
- grad_out_weight: float32 [5120, 2048], P(('replica', 'ctx', 'sub'), 'head'), parts along dimension 0
There are 2 independent parts, one for each index of `replica`. A program takes and returns all parts, laid end to end along the dimension named above; an argument that names none is the same for every part. Nothing has to cross between parts.
Inputs may be any that keep to these rules, and one draw needn't show every extreme that they name: segment numbers start at 0, never fall along the sequence and rise by one at the first token of each document; the last document's number is the max.
All inputs are finite; a program needn't handle non-finite values.
Results may differ from a plain program's by a relative error of at most 0.018.
Values may be sent and summed in bfloat16 or wider, within the bound.
A program may use at most 128 MiB of HBM per device.

v0:
```python
import jax
import jax.numpy as jnp
from jax import lax
from jax.sharding import PartitionSpec as P

DH = 256
WINDOW = 1024


def passed_along(shard, axis, by):
    devices = lax.axis_size(axis)
    pairs = [(i, i + by) for i in range(devices) if 0 <= i + by < devices]
    return lax.ppermute(shard, axis, pairs)


def shards(queries, keys, values, segment, cotangent, out_weight):
    row_count = queries.shape[0]
    kv_count = keys.shape[1] // DH
    groups = queries.shape[1] // keys.shape[1]
    devices = lax.axis_size(("ctx", "sub"))
    own_index = lax.axis_index(("ctx", "sub"))
    halo_rows = min(row_count, WINDOW)
    hop_count = (WINDOW + row_count - 1) // row_count
    score_scale = DH ** (-0.5)
    outgoing = (keys, values, segment)
    received = []
    for distance in range(1, hop_count + 1):
        received.append(
            passed_along((outgoing[0], outgoing[1], outgoing[2]), ("ctx", "sub"), distance)
        )
    ordered = received[::-1]
    all_keys = jnp.concatenate([item[0] for item in ordered] + [keys], 0)
    all_values = jnp.concatenate([item[1] for item in ordered] + [values], 0)
    all_segments = jnp.concatenate([item[2] for item in ordered] + [segment], 0)
    halo_offsets = jnp.arange(halo_rows, dtype=jnp.int32)
    key_pos = jnp.concatenate(
        [
            (own_index - distance) * row_count + row_count - halo_rows + halo_offsets
            for distance in range(hop_count, 0, -1)
        ]
        + [own_index * row_count + jnp.arange(row_count, dtype=jnp.int32)],
        0,
    )
    query_pos = own_index * row_count + jnp.arange(row_count, dtype=jnp.int32)
    allowed = (key_pos[None, :] >= 0) & (key_pos[None, :] <= query_pos[:, None])
    allowed = allowed & (query_pos[:, None] - key_pos[None, :] < WINDOW)
    allowed = allowed & (segment[:, None] == all_segments[None, :])
    key_total = all_keys.shape[0]
    query_heads = queries.reshape(row_count, kv_count, groups, DH)
    key_heads = all_keys.reshape(key_total, kv_count, DH)
    value_heads = all_values.reshape(key_total, kv_count, DH)
    scores = (
        jnp.einsum("qkgd,skd->kgqs", query_heads, key_heads, preferred_element_type=jnp.float32)
        * score_scale
    )
    scores = jnp.where(allowed[None, None], scores, -jnp.inf)
    row_max = jnp.max(scores, axis=-1, keepdims=True)
    log_total = row_max + jnp.log(jnp.sum(jnp.exp(scores - row_max), axis=-1, keepdims=True))
    softmax = jnp.exp(scores - log_total)
    rounded_softmax = softmax.astype(jnp.bfloat16)
    attention = jnp.einsum(
        "kgqs,skd->qkgd", rounded_softmax, value_heads, preferred_element_type=jnp.float32
    ).astype(jnp.bfloat16)
    attention_grad = jnp.dot(cotangent, out_weight, preferred_element_type=jnp.float32).astype(
        jnp.bfloat16
    )
    attention_grad = attention_grad.reshape(row_count, kv_count, groups, DH)
    row_dot = jnp.transpose(
        jnp.sum(attention.astype(jnp.float32) * attention_grad.astype(jnp.float32), axis=-1),
        (1, 2, 0),
    )
    softmax_grad = jnp.einsum(
        "qkgd,skd->kgqs", attention_grad, value_heads, preferred_element_type=jnp.float32
    )
    score_grad = (softmax * (softmax_grad - row_dot[..., None])).astype(jnp.bfloat16)
    query_grad = (
        jnp.einsum("kgqs,skd->qkgd", score_grad, key_heads, preferred_element_type=jnp.float32)
        * score_scale
    ).astype(jnp.bfloat16)
    key_terms = (
        jnp.einsum("kgqs,qkgd->skd", score_grad, query_heads, preferred_element_type=jnp.float32)
        * score_scale
    )
    value_terms = jnp.einsum(
        "kgqs,qkgd->skd", rounded_softmax, attention_grad, preferred_element_type=jnp.float32
    )
    key_terms = key_terms.reshape(key_total, kv_count * DH)
    value_terms = value_terms.reshape(key_total, kv_count * DH)
    own_keys_grad = key_terms[key_total - row_count :]
    own_values_grad = value_terms[key_total - row_count :]
    tail_keys = own_keys_grad
    tail_values = own_values_grad
    for distance in range(1, hop_count + 1):
        offset = (hop_count - distance) * halo_rows
        returned = passed_along(
            (key_terms[offset : offset + halo_rows], value_terms[offset : offset + halo_rows]),
            ("ctx", "sub"),
            -distance,
        )
        tail_keys = tail_keys + returned[0]
        tail_values = tail_values + returned[1]
    grad_keys = jnp.concatenate([own_keys_grad[: row_count - halo_rows], tail_keys], 0).astype(
        jnp.bfloat16
    )
    grad_values = jnp.concatenate(
        [own_values_grad[: row_count - halo_rows], tail_values], 0
    ).astype(jnp.bfloat16)
    attention_flat = attention.reshape(row_count, kv_count * groups * DH)
    token_norm = (row_count * devices) ** (-0.5)
    summed = lax.psum_scatter(
        lax.dot_general(
            cotangent, attention_flat, (((0,), (0,)), ((), ())), preferred_element_type=jnp.float32
        ),
        ("ctx", "sub"),
        scatter_dimension=0,
        tiled=True,
    )
    grad_out_weight = summed * token_norm
    return (
        query_grad.reshape(row_count, kv_count * groups * DH),
        grad_keys,
        grad_values,
        grad_out_weight,
    )


def solution(mesh):
    return jax.shard_map(
        shards,
        mesh=mesh,
        in_specs=(
            P(("replica", "ctx", "sub"), "head"),
            P(("replica", "ctx", "sub"), "head"),
            P(("replica", "ctx", "sub"), "head"),
            P(("replica", "ctx", "sub")),
            P(("replica", "ctx", "sub"), None),
            P(None, "head"),
        ),
        out_specs=(
            P(("replica", "ctx", "sub"), "head"),
            P(("replica", "ctx", "sub"), "head"),
            P(("replica", "ctx", "sub"), "head"),
            P(("replica", "ctx", "sub"), "head"),
        ),
        check_vma=False,
    )
```

profile of v0, /device:TPU:22, one launch (start us, length us, event | category | flops | bytes accessed | tf_op | source)
XLA Modules:
  0.0 263.2 jit_solution(10172741786797178557)
XLA Ops:
  7.2 0.0 copy-start
  7.2 0.0 reduce-scatter.4.cloned.1.call-start
  7.2 2.2 copy.54
  9.4 1.9 collective-permute-start.1
  11.3 3.5 %collective-permute-start = (bf16[512,512]{0,1:T(8,128)(2,1)}, bf16[512,512]{0,1:T(8,128)(2,1)}, u32[]{:S(2)}, u32[]{:S(2)}) collective-permute-start(bf16[512,512]{0,1:T(8,128)(2,1)} %copy.54), channel_id=1, source_target_pairs={{0,4},{1,5},{4,8},{5,9},{8,12},{9,13},{2,6},{3,7},{6,10},{7,11},{1... | collective-permute-start | bytes 1572872 | tf_op jit(solution)/shard_map/ppermute | solution.py:13
  14.8 2.0 collective-permute-start.3
  16.9 1.9 collective-permute-start.2
  18.8 2.0 copy.59
  20.9 1.9 collective-permute-start.5
  22.8 0.0 copy-done
  22.8 6.3 %convolution_convert_fusion.1 = bf16[512,1024]{1,0:T(8,128)(2,1)} fusion(bf16[512,2560]{1,0:T(8,128)(2,1)S(1)} %copy-done, bf16[2560,1024]{1,0:T(8,128)(2,1)} %param.11), kind=kOutput, calls=%fused_computation.21 | convolution fusion | flops 2684878848 | bytes 8912896 | tf_op jit(solution)/shard_map/dot_general | solution.py:64
  29.2 2.3 copy.95
  31.5 2.3 copy.96
  33.7 0.0 collective-permute-done.3
  33.7 2.2 collective-permute-start.4
  36.0 0.0 collective-permute-done.2
  36.0 0.0 copy-done.10
  36.0 1.7 fusion.7
  37.7 0.0 collective-permute-done.1
  37.7 0.0 collective-permute-done
  37.7 1.5 pad_maximum_fusion
  39.2 0.0 copy-start.6
  39.2 0.0 copy-done.4
  39.2 2.4 fusion.3
  41.6 0.0 copy-done.6
  41.6 0.0 copy-start.2
  41.6 2.7 %exponential_reduce_fusion = f32[2,2,512]{2,1,0:T(2,128)S(1)} fusion(f32[2,1536,512,2]{2,1,3,0:T(8,128)S(1)} %get-tuple-element.23, f32[2,2,512]{2,1,0:T(2,128)S(1)} %get-tuple-element.22, pred[512,1536]{0,1:T(8,128)(4,1)S(1)} %fusion.7), kind=kLoop, calls=%fused_computation.5 | loop fusion | flops 12580864 | bytes 13385728 | tf_op jit(solution)/shard_map/reduce_sum | solution.py:58
  44.4 0.0 copy-start.9
  44.4 0.0 collective-permute-done.5
  44.4 5.8 %collective-permute-done.4 = bf16[512,512]{0,1:T(8,128)(2,1)S(1)} collective-permute-done((bf16[512,512]{0,1:T(8,128)(2,1)}, bf16[512,512]{0,1:T(8,128)(2,1)S(1)}, u32[]{:S(2)}, u32[]{:S(2)}) %collective-permute-start.4) | collective-permute-done | bytes 524320 | tf_op jit(solution)/shard_map/ppermute | solution.py:13
  50.2 1.3 pad_maximum_fusion.1
  51.5 0.0 copy-start.7
  51.5 3.9 %multiply_reduce_fusion = (f32[512,2,2]{0,2,1:T(2,128)S(1)}, bf16[2,256,2,512]{3,1,2,0:T(8,128)(2,1)S(1)}) fusion(bf16[512,1024]{0,1:T(8,128)(2,1)S(1)} %copy-done.9, bf16[1536,2,256,1]{0,2,3,1:T(8,128)(2,1)S(1)} %bitcast.94, f32[2,1536,512,2]{2,1,3,0:T(8,128)S(1)} %get-tuple-element.23, f32[2,2,512]{2,1,0:T(2,128)S(1)} %log_add_fusion, ...), kind=kOutput, calls=%fused_computation.17 | convolution fusion | flops 1625815040 | bytes 17055744 | tf_op jit(solution)/shard_map/kgqs,skd->qkgd/dot_general | solution.py:61
  55.4 5.5 %convolution_bitcast_fusion = f32[2560,1024]{0,1:T(8,128)} fusion(bf16[512,1024]{0,1:T(8,128)(2,1)S(1)} %bitcast.99, bf16[512,2560]{1,0:T(8,128)(2,1)S(1)} %copy-done), kind=kOutput, calls=%fused_computation.8 | convolution fusion | flops 2684354560 | bytes 14155776 | tf_op jit(solution)/shard_map/dot_general | solution.py:111
  60.9 11.4 %copy.93 = f32[2560,1024]{1,0:T(8,128)} copy(f32[2560,1024]{0,1:T(8,128)} %convolution_bitcast_fusion) | data formatting | bytes 20971520
  72.3 0.0 reduce-scatter.4.cloned.1.call-update
  72.3 1.4 copy-done.8
  73.7 7.5 %fusion.1 = bf16[2,2,512,1536]{2,3,1,0:T(8,128)(2,1)S(1)} fusion(f32[2,1536,512,2]{2,1,3,0:T(8,128)} %copy-done.2, bf16[1536,2,256,1]{0,2,3,1:T(8,128)(2,1)S(1)} %bitcast.95, bf16[512,2,2,256]{0,3,2,1:T(8,128)(2,1)} %bitcast.96, f32[2,2,512]{2,1,0:T(2,128)S(1)} %bitcast.100, f32[2,2,512]{2,1,0:T(2,128)S(1)} %log_add_fusion, pred[512,1536]{0,1:T(8,128)(4,1)S(1)} %fusion.7), kind=kOutput, calls=%fused_computation.2 | convolution fusion | flops 1629487104 | bytes 22298624 | tf_op jit(solution)/shard_map/qkgd,skd->kgqs/dot_general | solution.py:72
  81.2 1.8 fusion.5
  83.1 0.8 copy-done.3
  83.9 1.4 fusion.11
  85.3 2.5 copy.71
  87.9 4.2 %collective-permute-start.7 = (f32[512,512]{1,0:T(8,128)}, f32[512,512]{1,0:T(8,128)}, u32[]{:S(2)}, u32[]{:S(2)}) collective-permute-start(f32[512,512]{1,0:T(8,128)} %copy.71), channel_id=1, source_target_pairs={{4,0},{5,1},{8,4},{9,5},{12,8},{13,9},{6,2},{7,3},{10,6},{11,7},{1... | collective-permute-start | bytes 3145736 | tf_op jit(solution)/shard_map/ppermute | solution.py:13
  92.0 1.3 copy.69
  93.4 2.1 collective-permute-start.6
  95.5 7.0 %convolution_bitcast_fusion.1 = f32[1536,2,256]{0,2,1:T(8,128)S(1)} fusion(bf16[512,2,2,256]{0,3,2,1:T(8,128)(2,1)} %bitcast.97, f32[2,1536,512,2]{2,1,3,0:T(8,128)} %copy-done.2, f32[2,2,512]{2,1,0:T(2,128)S(1)} %log_add_fusion, pred[512,1536]{0,1:T(8,128)(4,1)S(1)} %fusion.7), kind=kOutput, calls=%fused_computation.9 | convolution fusion | flops 1623195648 | bytes 17571840 | tf_op jit(solution)/shard_map/kgqs,qkgd->skd/dot_general | solution.py:84
  102.5 1.7 fusion.10
  104.2 2.6 copy.76
  106.7 1.9 collective-permute-start.9
  108.7 1.3 copy.74
  110.0 2.2 collective-permute-start.8
  112.2 5.1 %multiply_convert_fusion = bf16[2,256,2,512]{3,1,2,0:T(8,128)(2,1)S(1)} fusion(bf16[1536,2,256,1]{0,2,3,1:T(8,128)(2,1)} %bitcast.93, bf16[2,2,512,1536]{2,3,1,0:T(8,128)(2,1)} %copy-done.3), kind=kOutput, calls=%fused_computation.16 | convolution fusion | flops 1611661312 | bytes 8912896 | tf_op jit(solution)/shard_map/kgqs,skd->qkgd/dot_general | solution.py:77
  117.2 1.3 copy.77
  118.5 0.3 copy.70
  118.9 1.6 copy.75
  120.4 18.1 %collective-permute-done.7 = f32[512,512]{1,0:T(8,128)} collective-permute-done((f32[512,512]{1,0:T(8,128)}, f32[512,512]{1,0:T(8,128)}, u32[]{:S(2)}, u32[]{:S(2)}) %collective-permute-start.7) | collective-permute-done | bytes 1048608 | tf_op jit(solution)/shard_map/ppermute | solution.py:13
  138.5 43.6 %collective-permute-done.6 = f32[512,512]{1,0:T(8,128)} collective-permute-done((f32[512,512]{1,0:T(8,128)}, f32[512,512]{1,0:T(8,128)}, u32[]{:S(2)}, u32[]{:S(2)}) %collective-permute-start.6) | collective-permute-done | bytes 1048608 | tf_op jit(solution)/shard_map/ppermute | solution.py:13
  182.1 2.6 add_convert_fusion.1
  184.7 32.0 %collective-permute-done.9 = f32[512,512]{1,0:T(8,128)} collective-permute-done((f32[512,512]{1,0:T(8,128)}, f32[512,512]{1,0:T(8,128)}, u32[]{:S(2)}, u32[]{:S(2)}) %collective-permute-start.9) | collective-permute-done | bytes 1048608 | tf_op jit(solution)/shard_map/ppermute | solution.py:13
  216.7 28.3 %collective-permute-done.8 = f32[512,512]{1,0:T(8,128)} collective-permute-done((f32[512,512]{1,0:T(8,128)}, f32[512,512]{1,0:T(8,128)}, u32[]{:S(2)}, u32[]{:S(2)}) %collective-permute-start.8) | collective-permute-done | bytes 1048608 | tf_op jit(solution)/shard_map/ppermute | solution.py:13
  245.0 2.6 add_convert_fusion
  247.6 3.1 %copy.94 = f32[320,1024]{0,1:T(8,128)} copy(f32[320,1024]{1,0:T(8,128)} %reduce-scatter.4.cloned.1.call-done) | data formatting | bytes 2621440
  250.7 2.7 %broadcast_multiply_fusion = f32[320,1024]{0,1:T(8,128)} fusion(f32[320,1024]{0,1:T(8,128)} %copy.94), kind=kLoop, calls=%fused_computation.24 | loop fusion | flops 327680 | bytes 2621440 | tf_op jit(solution)/shard_map/mul | solution.py:118
  253.4 2.9 %copy.78 = f32[320,1024]{1,0:T(8,128)} copy(f32[320,1024]{0,1:T(8,128)} %broadcast_multiply_fusion) | data formatting | bytes 2621440
  (18 shorter events, 0.1 us)
Async XLA Ops:
  7.2 15.6 %copy-start = (bf16[512,2560]{1,0:T(8,128)(2,1)S(1)}, bf16[512,2560]{1,0:T(8,128)(2,1)}, u32[]{:S(2)}) copy-start(bf16[512,2560]{1,0:T(8,128)(2,1)} %param.10) | copy-start | bytes 7864324
  7.2 240.4 %reduce-scatter.4.cloned.1.call-start = ((), (), s32[]{:S(2)}) async-start(), calls=%async_computation.1 | async-start | bytes 11796480
  9.4 28.3 %collective-permute-start.1 = (bf16[512,512]{0,1:T(8,128)(2,1)}, bf16[512,512]{0,1:T(8,128)(2,1)}, u32[]{:S(2)}, u32[]{:S(2)}) collective-permute-start(bf16[512,512]{0,1:T(8,128)(2,1)} %copy.54), channel_id=1, source_target_pairs={{0,1},{1,4},{4,5},{5,8},{8,9},{9,12},{12,13},{2,3},{3,6},{6,7},{7,... | collective-permute-start | bytes 1572872 | tf_op jit(solution)/shard_map/ppermute | solution.py:13
  11.3 26.4 %collective-permute-start = (bf16[512,512]{0,1:T(8,128)(2,1)}, bf16[512,512]{0,1:T(8,128)(2,1)}, u32[]{:S(2)}, u32[]{:S(2)}) collective-permute-start(bf16[512,512]{0,1:T(8,128)(2,1)} %copy.54), channel_id=1, source_target_pairs={{0,4},{1,5},{4,8},{5,9},{8,12},{9,13},{2,6},{3,7},{6,10},{7,11},{1... | collective-permute-start | bytes 1572872 | tf_op jit(solution)/shard_map/ppermute | solution.py:13
  14.8 18.9 %collective-permute-start.3 = (s32[512]{0:T(512)}, s32[512]{0:T(512)S(1)}, u32[]{:S(2)}, u32[]{:S(2)}) collective-permute-start(s32[512]{0:T(512)} %param.9), channel_id=1, source_target_pairs={{0,1},{1,4},{4,5},{5,8},{8,9},{9,12},{12,13},{2,3},{3,6},{6,7},{7,... | collective-permute-start | bytes 6152 | tf_op jit(solution)/shard_map/ppermute | solution.py:13
  16.9 19.1 %collective-permute-start.2 = (s32[512]{0:T(512)}, s32[512]{0:T(512)S(1)}, u32[]{:S(2)}, u32[]{:S(2)}) collective-permute-start(s32[512]{0:T(512)} %param.9), channel_id=1, source_target_pairs={{0,4},{1,5},{4,8},{5,9},{8,12},{9,13},{2,6},{3,7},{6,10},{7,11},{1... | collective-permute-start | bytes 6152 | tf_op jit(solution)/shard_map/ppermute | solution.py:13
  20.9 23.6 %collective-permute-start.5 = (bf16[512,512]{0,1:T(8,128)(2,1)}, bf16[512,512]{0,1:T(8,128)(2,1)}, u32[]{:S(2)}, u32[]{:S(2)}) collective-permute-start(bf16[512,512]{0,1:T(8,128)(2,1)} %copy.59), channel_id=1, source_target_pairs={{0,1},{1,4},{4,5},{5,8},{8,9},{9,12},{12,13},{2,3},{3,6},{6,7},{7,... | collective-permute-start | bytes 1572872 | tf_op jit(solution)/shard_map/ppermute | solution.py:13
  29.1 6.8 %copy-start.10 = (s32[512]{0:T(512)S(1)}, s32[512]{0:T(512)}, u32[]{:S(2)}) copy-start(s32[512]{0:T(512)} %param.9) | copy-start | bytes 6148
  33.7 5.5 %copy-start.4 = (bf16[512,1024]{0,1:T(8,128)(2,1)S(1)}, bf16[512,1024]{0,1:T(8,128)(2,1)}, u32[]{:S(2)}) copy-start(bf16[512,1024]{0,1:T(8,128)(2,1)} %copy.95) | copy-start | bytes 3145732
  33.7 16.4 %collective-permute-start.4 = (bf16[512,512]{0,1:T(8,128)(2,1)}, bf16[512,512]{0,1:T(8,128)(2,1)S(1)}, u32[]{:S(2)}, u32[]{:S(2)}) collective-permute-start(bf16[512,512]{0,1:T(8,128)(2,1)} %copy.59), channel_id=1, source_target_pairs={{0,4},{1,5},{4,8},{5,9},{8,12},{9,13},{2,6},{3,7},{6,10},{7,11},{1... | collective-permute-start | bytes 1572872 | tf_op jit(solution)/shard_map/ppermute | solution.py:13
  39.2 2.4 copy-start.6
  41.6 9.9 %copy-start.2 = (f32[2,1536,512,2]{2,1,3,0:T(8,128)}, f32[2,1536,512,2]{2,1,3,0:T(8,128)S(1)}, u32[]{:S(2)}) copy-start(f32[2,1536,512,2]{2,1,3,0:T(8,128)S(1)} %get-tuple-element.23) | copy-start | bytes 37748740
  44.4 7.2 %copy-start.9 = (bf16[512,1024]{0,1:T(8,128)(2,1)S(1)}, bf16[512,1024]{0,1:T(8,128)(2,1)}, u32[]{:S(2)}) copy-start(bf16[512,1024]{0,1:T(8,128)(2,1)} %copy.96) | copy-start | bytes 3145732
  51.5 3.9 %copy-start.7 = (bf16[1536,512]{0,1:T(8,128)(2,1)}, bf16[1536,512]{0,1:T(8,128)(2,1)S(1)}, u32[]{:S(2)}) copy-start(bf16[1536,512]{0,1:T(8,128)(2,1)S(1)} %pad_maximum_fusion.1) | copy-start | bytes 4718596
  72.3 1.4 copy-start.8
  73.7 7.5 %copy-start.5 = (bf16[512,1024]{0,1:T(8,128)(2,1)S(1)}, bf16[512,1024]{0,1:T(8,128)(2,1)}, u32[]{:S(2)}) copy-start(bf16[512,1024]{0,1:T(8,128)(2,1)} %copy.95) | copy-start | bytes 3145732
  81.2 2.6 %copy-start.3 = (bf16[2,2,512,1536]{2,3,1,0:T(8,128)(2,1)}, bf16[2,2,512,1536]{2,3,1,0:T(8,128)(2,1)S(1)}, u32[]{:S(2)}) copy-start(bf16[2,2,512,1536]{2,3,1,0:T(8,128)(2,1)S(1)} %fusion.1) | copy-start | bytes 18874372
  87.9 50.7 %collective-permute-start.7 = (f32[512,512]{1,0:T(8,128)}, f32[512,512]{1,0:T(8,128)}, u32[]{:S(2)}, u32[]{:S(2)}) collective-permute-start(f32[512,512]{1,0:T(8,128)} %copy.71), channel_id=1, source_target_pairs={{4,0},{5,1},{8,4},{9,5},{12,8},{13,9},{6,2},{7,3},{10,6},{11,7},{1... | collective-permute-start | bytes 3145736 | tf_op jit(solution)/shard_map/ppermute | solution.py:13
  93.4 88.7 %collective-permute-start.6 = (f32[512,512]{1,0:T(8,128)}, f32[512,512]{1,0:T(8,128)}, u32[]{:S(2)}, u32[]{:S(2)}) collective-permute-start(f32[512,512]{1,0:T(8,128)} %copy.69), channel_id=1, source_target_pairs={{1,0},{4,1},{5,4},{8,5},{9,8},{12,9},{13,12},{3,2},{6,3},{7,6},{10... | collective-permute-start | bytes 3145736 | tf_op jit(solution)/shard_map/ppermute | solution.py:13
  106.7 110.0 %collective-permute-start.9 = (f32[512,512]{1,0:T(8,128)}, f32[512,512]{1,0:T(8,128)}, u32[]{:S(2)}, u32[]{:S(2)}) collective-permute-start(f32[512,512]{1,0:T(8,128)} %copy.76), channel_id=1, source_target_pairs={{4,0},{5,1},{8,4},{9,5},{12,8},{13,9},{6,2},{7,3},{10,6},{11,7},{1... | collective-permute-start | bytes 3145736 | tf_op jit(solution)/shard_map/ppermute | solution.py:13
  110.0 135.0 %collective-permute-start.8 = (f32[512,512]{1,0:T(8,128)}, f32[512,512]{1,0:T(8,128)}, u32[]{:S(2)}, u32[]{:S(2)}) collective-permute-start(f32[512,512]{1,0:T(8,128)} %copy.74), channel_id=1, source_target_pairs={{1,0},{4,1},{5,4},{8,5},{9,8},{12,9},{13,12},{3,2},{6,3},{7,6},{10... | collective-permute-start | bytes 3145736 | tf_op jit(solution)/shard_map/ppermute | solution.py:13
  247.6 8.7 %copy-start.1 = (bf16[512,2560]{1,0:T(8,128)(2,1)S(1)}, bf16[512,2560]{1,0:T(8,128)(2,1)}, u32[]{:S(2)}) copy-start(bf16[512,2560]{1,0:T(8,128)(2,1)} %param.10) | copy-start | bytes 7864324
Sparse Core Ops, SparseCore 0:
  72.4 170.5 reduce-scatter.3
where the time goes:
time: 267 us; the launch traced here: 263 us
  waiting for transfers between devices  128 us (48%)
  local copies, waits for them, and re-layouts  42.6 us (16%)
  matrix products  39.4 us (15%)
  starting transfers between devices  23.9 us (9%)
  other arithmetic  15.1 us (6%)
  between operations  14.4 us (5%)
    ppermute x10, waiting for transfers between devices, passed_along(): return lax.ppermute(shard, axis, pairs)  128 us
    unnamed x28, local copies, waits for them, and re-layouts  25.2 us
    ppermute x10, starting transfers between devices, passed_along(): return lax.ppermute(shard, axis, pairs)  23.9 us
    dot_general x1, matrix products, shards(): jnp.einsum('qkgd,skd->kgqs', attention_grad, value_heads, preferred_eleme...  7.51 us
    dot_general x1, matrix products, shards(): jnp.einsum('kgqs,qkgd->skd', rounded_softmax, attention_grad, preferred_e...  6.98 us
    dot_general x1, matrix products, shards(): jnp.dot(cotangent, out_weight, preferred_element_type=jnp.float32)  6.33 us
    slice x3, local copies, waits for them, and re-layouts, shards(): value_terms[offset:offset + halo_rows]  5.57 us
    dot_general x1, matrix products, shards(): lax.dot_general(cotangent, attention_flat, (((0,), (0,)), ((), ())), pref...  5.45 us
  transfers between devices with their start and end apart: 11, of which 5 were waited for; matrix products, arithmetic and copies ran while one was open for 24% of the time, Pallas kernels for 0%

commit v1 on v0

v1 whole, which is shorter than its diff:
```python
import functools

import jax
import jax.numpy as jnp
from jax import lax
from jax.experimental import pallas as pl
from jax.experimental.pallas import tpu as pltpu
from jax.sharding import PartitionSpec as P

DH = 256
WINDOW = 1024
QB = 256
SPAN = WINDOW + QB
MASKED = -1e30
MESH = pl.DeviceIdType.MESH
F32 = jnp.float32
BF16 = jnp.bfloat16


def dot_nt(a, b):
    return lax.dot_general(a, b, (((1,), (1,)), ((), ())), preferred_element_type=F32)


def dot_tn(a, b):
    return lax.dot_general(a, b, (((0,), (0,)), ((), ())), preferred_element_type=F32)


def dot_nn(a, b):
    return lax.dot_general(a, b, (((1,), (0,)), ((), ())), preferred_element_type=F32)


def layer_kernel(
    nz, ng, groups, norm,
    q_hbm, k_hbm, v_hbm, seg_hbm, cot_hbm, w_hbm,
    dq_ref, dk_ref, dv_ref, gow_ref,
    q_s, w_s, cot_s, cot_t, da_s, at_s, kall, vall, seg_s, bias_s, prob_s, dk_acc, dv_acc,
    mid_send, mid_recv, back_send, back_recv,
    own_part, pair_send, pair_recv, far_send, far_recv, own_sum,
    in_sem, halo_ss, halo_rs, fwd_ss, fwd_rs, mid_ss, mid_rs, back_ss, back_rs,
    pair_ss, pair_rs, far_ss, far_rs,
):
    heads = ng * groups
    rows = q_hbm.shape[0]
    width = cot_hbm.shape[1]
    part = width // (2 * nz)
    scale = DH ** -0.5
    z = lax.axis_index("ctx")
    s = lax.axis_index("sub")
    peer = 1 - s
    above = lax.rem(z + 1, nz)
    below = lax.rem(z + nz - 1, nz)
    has_above = z < nz - 1
    has_below = z > 0

    def cols(h):
        return pl.ds(h * DH, DH)

    loads = []

    def load(src, dst):
        copy = pltpu.make_async_copy(src, dst, in_sem.at[len(loads)])
        copy.start()
        loads.append(copy)
        return copy

    load_seg = load(seg_hbm, seg_s.at[2])
    load_cot = load(cot_hbm, cot_s)
    load_w = [load(w_hbm.at[:, cols(h)], w_s.at[h]) for h in range(heads)]
    load_kv = [
        (
            load(k_hbm.at[:, cols(g)], kall.at[g, pl.ds(2 * rows, rows)]),
            load(v_hbm.at[:, cols(g)], vall.at[g, pl.ds(2 * rows, rows)]),
        )
        for g in range(ng)
    ]
    load_q = [load(q_hbm.at[:, cols(h)], q_s.at[h]) for h in range(heads)]

    barrier = pltpu.get_barrier_semaphore()
    for step in range(1, nz):
        pl.semaphore_signal(barrier, inc=1, device_id={"ctx": lax.rem(z + step, nz)}, device_id_type=MESH)
    pl.semaphore_signal(barrier, inc=1, device_id={"sub": peer}, device_id_type=MESH)
    pl.semaphore_wait(barrier, nz)

    def halo(i, src, dst):
        return pltpu.make_async_remote_copy(
            src_ref=src, dst_ref=dst, send_sem=halo_ss.at[i], recv_sem=halo_rs.at[i],
            device_id={"ctx": above}, device_id_type=MESH,
        )

    def forward(i, src, dst):
        return pltpu.make_async_remote_copy(
            src_ref=src, dst_ref=dst, send_sem=fwd_ss.at[i], recv_sem=fwd_rs.at[i],
            device_id={"sub": peer}, device_id_type=MESH,
        )

    first, middle = pl.ds(0, rows), pl.ds(rows, rows)
    seg_i = 2 * ng
    halos = [halo(seg_i, seg_hbm, seg_s.at[0])]
    from_own = [forward(seg_i, seg_hbm, seg_s.at[1])]
    from_halo = [forward(seg_i, seg_s.at[0], seg_s.at[1])]
    for g in range(ng):
        for j, (hbm, both) in enumerate(((k_hbm, kall), (v_hbm, vall))):
            i = 2 * g + j
            halos.append(halo(i, hbm.at[:, cols(g)], both.at[g, first]))
            from_own.append(forward(i, hbm.at[:, cols(g)], both.at[g, middle]))
            from_halo.append(forward(i, both.at[g, first], both.at[g, middle]))

    @pl.when(has_above)
    def _():
        for copy in halos:
            copy.start()

    @pl.when(s == 0)
    def _():
        for copy in from_own:
            copy.start()

    @pl.when(jnp.logical_not(has_below))
    def _():
        seg_s[0] = jnp.full((1, rows), -1, jnp.int32)
        for g in range(ng):
            kall[g, first] = jnp.zeros((rows, DH), BF16)
            vall[g, first] = jnp.zeros((rows, DH), BF16)

    @pl.when(jnp.logical_not(has_below) & (s == 0))
    def _():
        seg_s[1] = jnp.full((1, rows), -1, jnp.int32)
        for g in range(ng):
            kall[g, middle] = jnp.zeros((rows, DH), BF16)
            vall[g, middle] = jnp.zeros((rows, DH), BF16)

    def arrive(indices):
        @pl.when(has_below)
        def _():
            for i in indices:
                halos[i].wait_recv()

        @pl.when(has_below & (s == 1))
        def _():
            for i in indices:
                from_halo[i].start()

        @pl.when(has_below | (s == 1))
        def _():
            for i in indices:
                from_halo[i].wait_recv()

    load_cot.wait()
    for h in range(heads):
        load_w[h].wait()

    def attention_grad(h, carry):
        da_s[h] = dot_nn(cot_s[...], w_s[h]).astype(BF16)
        return carry

    lax.fori_loop(0, heads, attention_grad, 0)

    for j in range(width // DH):
        cot_t[pl.ds(j * DH, DH)] = cot_s[:, cols(j)].T

    load_seg.wait()
    arrive([0])
    for b in range(rows // QB):
        own = seg_s[2]
        keys_row = jnp.concatenate([seg_s[0], seg_s[1], own], axis=1)[:, b * QB : b * QB + SPAN]
        column = jnp.broadcast_to(own[:, b * QB : (b + 1) * QB].astype(F32), (128, QB)).T[:, :1]
        at_query = lax.broadcasted_iota(jnp.int32, (QB, SPAN), 0)
        at_key = lax.broadcasted_iota(jnp.int32, (QB, SPAN), 1)
        allowed = (at_key > at_query) & (at_key <= at_query + WINDOW)
        allowed = allowed & (column == keys_row.astype(F32))
        bias_s[b] = jnp.where(allowed, 0.0, MASKED)

    def mid_copy(g, j):
        return pltpu.make_async_remote_copy(
            src_ref=mid_send.at[g, j], dst_ref=mid_recv.at[g, j],
            send_sem=mid_ss.at[g, j], recv_sem=mid_rs.at[g, j],
            device_id={"sub": peer}, device_id_type=MESH,
        )

    def back_copy(g, j):
        return pltpu.make_async_remote_copy(
            src_ref=back_send.at[g, j], dst_ref=back_recv.at[g, j],
            send_sem=back_ss.at[g, j], recv_sem=back_rs.at[g, j],
            device_id={"ctx": below}, device_id_type=MESH,
        )

    def pair_copy(h):
        return pltpu.make_async_remote_copy(
            src_ref=pair_send.at[h], dst_ref=pair_recv.at[h],
            send_sem=pair_ss.at[h], recv_sem=pair_rs.at[h],
            device_id={"sub": peer}, device_id_type=MESH,
        )

    def far_send_copy(h, d):
        return pltpu.make_async_remote_copy(
            src_ref=far_send.at[h, d], dst_ref=far_recv.at[h, z],
            send_sem=far_ss.at[h, d], recv_sem=far_rs.at[h, z],
            device_id={"ctx": d}, device_id_type=MESH,
        )

    def far_recv_copy(h, d):
        return pltpu.make_async_remote_copy(
            src_ref=far_send.at[h, d], dst_ref=far_recv.at[h, d],
            send_sem=far_ss.at[h, d], recv_sem=far_rs.at[h, d],
            device_id={"ctx": d}, device_id_type=MESH,
        )

    def part_rows(d, side):
        return pl.ds(pl.multiple_of((d * 2 + side) * part, 16), part)

    def send_back(g):
        for j, acc in enumerate((dk_acc, dv_acc)):
            mid_copy(g, j).wait_recv()
            other = mid_recv[g, j].astype(F32)
            back_send[g, j] = (acc[g, first] + jnp.where(s == 1, other, 0.0)).astype(BF16)

            @pl.when(has_below)
            def _():
                back_copy(g, j).start()

            last = pl.ds(2 * rows, rows)
            acc[g, last] = acc[g, last] + jnp.where(s == 0, other, 0.0)

    for g in range(ng):
        load_kv[g][0].wait()
        load_kv[g][1].wait()
        arrive([1 + 2 * g, 2 + 2 * g])
        dk_acc[g] = jnp.zeros((3 * rows, DH), F32)
        dv_acc[g] = jnp.zeros((3 * rows, DH), F32)
        for h in range(g * groups, (g + 1) * groups):
            load_q[h].wait()

            def attend(b, carry):
                mine = pl.ds(pl.multiple_of(b * QB, QB), QB)
                reach = pl.ds(pl.multiple_of(b * QB, QB), SPAN)
                scores = dot_nt(q_s[h, mine], kall[g, reach]) * scale + bias_s[b]
                top = jnp.max(scores, axis=1, keepdims=True)
                raised = jnp.exp(scores - top)
                probs = raised * (1.0 / jnp.sum(raised, axis=1, keepdims=True))
                prob_s[b] = probs
                at_s[mine] = dot_nn(probs.astype(BF16), vall[g, reach]).astype(BF16)
                return carry

            lax.fori_loop(0, rows // QB, attend, 0)

            def weight_part(d, carry):
                pair_send[h, d] = dot_nn(cot_t[part_rows(d, peer)], at_s[...]).astype(BF16)
                return carry

            lax.fori_loop(0, nz, weight_part, 0)
            pair_copy(h).start()

            def weight_own(d, carry):
                own_part[d] = dot_nn(cot_t[part_rows(d, s)], at_s[...])
                return carry

            lax.fori_loop(0, nz, weight_own, 0)

            def attend_back(b, carry):
                mine = pl.ds(pl.multiple_of(b * QB, QB), QB)
                reach = pl.ds(pl.multiple_of(b * QB, QB), SPAN)
                grad = da_s[h, mine]
                probs = prob_s[b]
                delta = jnp.sum(at_s[mine].astype(F32) * grad.astype(F32), axis=1, keepdims=True)
                dscores = (probs * (dot_nt(grad, vall[g, reach]) - delta)).astype(BF16)
                dq_ref[mine, cols(h)] = (dot_nn(dscores, kall[g, reach]) * scale).astype(BF16)
                dk_acc[g, reach] += dot_tn(dscores, q_s[h, mine])
                dv_acc[g, reach] += dot_tn(probs.astype(BF16), grad)
                return carry

            lax.fori_loop(0, rows // QB, attend_back, 0)

            pair_copy(h).wait_recv()

            def pair_sum(d, carry):
                total = own_part[d] + pair_recv[h, d].astype(F32)
                own_part[d] = total
                far_send[h, d] = total.astype(BF16)
                return carry

            lax.fori_loop(0, nz, pair_sum, 0)
            own_sum[h] = own_part[z]
            for step in range(1, nz):
                far_send_copy(h, lax.rem(z + step, nz)).start()
            if h == g * groups and g > 0:
                send_back(g - 1)

        for j, acc in enumerate((dk_acc, dv_acc)):
            mid_send[g, j] = acc[g, middle].astype(BF16)
            mid_copy(g, j).start()
    send_back(ng - 1)

    for h in range(heads):
        for step in range(1, nz):
            far_recv_copy(h, lax.rem(z + step, nz)).wait_recv()
        total = own_sum[h]
        for step in range(1, nz):
            total = total + far_recv[h, lax.rem(z + step, nz)].astype(F32)
        gow_ref[:, cols(h)] = total * norm

    last = pl.ds(2 * rows, rows)

    @pl.when(jnp.logical_not(has_above))
    def _():
        for g in range(ng):
            dk_ref[:, cols(g)] = (dk_acc[g, last] * scale).astype(BF16)
            dv_ref[:, cols(g)] = dv_acc[g, last].astype(BF16)

    @pl.when(has_above)
    def _():
        for g in range(ng):
            back_copy(g, 0).wait_recv()
            dk_ref[:, cols(g)] = ((dk_acc[g, last] + back_recv[g, 0].astype(F32)) * scale).astype(BF16)
            back_copy(g, 1).wait_recv()
            dv_ref[:, cols(g)] = (dv_acc[g, last] + back_recv[g, 1].astype(F32)).astype(BF16)

    @pl.when(has_above)
    def _():
        for copy in halos:
            copy.wait_send()

    @pl.when(has_below | (s == 0))
    def _():
        for copy in from_halo:
            copy.wait_send()

    for g in range(ng):
        for j in range(2):
            mid_copy(g, j).wait_send()

            @pl.when(has_below)
            def _():
                back_copy(g, j).wait_send()

    for h in range(heads):
        pair_copy(h).wait_send()
        for step in range(1, nz):
            far_send_copy(h, lax.rem(z + step, nz)).wait_send()


def shards(nz, queries, keys, values, segment, cotangent, out_weight):
    rows = queries.shape[0]
    ng = keys.shape[1] // DH
    groups = queries.shape[1] // keys.shape[1]
    heads = ng * groups
    width = cotangent.shape[1]
    part = width // (2 * nz)
    norm = (rows * 2 * nz) ** (-0.5)
    kv_block = pltpu.VMEM((ng, 2, rows, DH), BF16)
    parts = pltpu.VMEM((heads, nz, part, DH), BF16)
    dma = pltpu.SemaphoreType.DMA
    return pl.pallas_call(
        functools.partial(layer_kernel, nz, ng, groups, norm),
        out_shape=(
            jax.ShapeDtypeStruct(queries.shape, BF16),
            jax.ShapeDtypeStruct(keys.shape, BF16),
            jax.ShapeDtypeStruct(values.shape, BF16),
            jax.ShapeDtypeStruct((part, heads * DH), F32),
        ),
        in_specs=[pl.BlockSpec(memory_space=pl.ANY)] * 6,
        out_specs=[pl.BlockSpec(memory_space=pltpu.VMEM)] * 4,
        scratch_shapes=[
            pltpu.VMEM((heads, rows, DH), BF16),
            pltpu.VMEM((heads, width, DH), BF16),
            pltpu.VMEM((rows, width), BF16),
            pltpu.VMEM((width, rows), BF16),
            pltpu.VMEM((heads, rows, DH), BF16),
            pltpu.VMEM((rows, DH), BF16),
            pltpu.VMEM((ng, 3 * rows, DH), BF16),
            pltpu.VMEM((ng, 3 * rows, DH), BF16),
            pltpu.VMEM((3, 1, rows), jnp.int32),
            pltpu.VMEM((rows // QB, QB, SPAN), F32),
            pltpu.VMEM((rows // QB, QB, SPAN), F32),
            pltpu.VMEM((ng, 3 * rows, DH), F32),
            pltpu.VMEM((ng, 3 * rows, DH), F32),
            kv_block, kv_block, kv_block, kv_block,
            pltpu.VMEM((nz, part, DH), F32),
            parts, parts, parts, parts,
            pltpu.VMEM((heads, part, DH), F32),
            dma((2 + 2 * heads + 2 * ng,)),
            dma((2 * ng + 1,)), dma((2 * ng + 1,)),
            dma((2 * ng + 1,)), dma((2 * ng + 1,)),
            dma((ng, 2)), dma((ng, 2)),
            dma((ng, 2)), dma((ng, 2)),
            dma((heads,)), dma((heads,)),
            dma((heads, nz)), dma((heads, nz)),
        ],
        compiler_params=pltpu.CompilerParams(
            collective_id=0, has_side_effects=True, vmem_limit_bytes=60 * 1024 * 1024
        ),
    )(queries, keys, values, segment.reshape(1, rows), cotangent, out_weight)


def solution(mesh):
    return jax.shard_map(
        functools.partial(shards, mesh.shape["ctx"]),
        mesh=mesh,
        in_specs=(
            P(("replica", "ctx", "sub"), "head"),
            P(("replica", "ctx", "sub"), "head"),
            P(("replica", "ctx", "sub"), "head"),
            P(("replica", "ctx", "sub")),
            P(("replica", "ctx", "sub"), None),
            P(None, "head"),
        ),
        out_specs=(
            P(("replica", "ctx", "sub"), "head"),
            P(("replica", "ctx", "sub"), "head"),
            P(("replica", "ctx", "sub"), "head"),
            P(("replica", "ctx", "sub"), "head"),
        ),
        check_vma=False,
    )
```

time: 267 us -> 113 us (0.42)
  the two profiles are of different devices: /device:TPU:22 before, /device:TPU:15 now
where the time goes in v1:
time: 113 us
  Pallas kernels  106 us (94%)
  local copies, waits for them, and re-layouts  6.12 us (5%)
    pallas_call x1, Pallas kernels, shards(): pl.pallas_call(functools.partial(layer_kernel, nz, ng, groups, norm), out...  106 us
    unnamed x8, local copies, waits for them, and re-layouts  6.12 us

profile of v1, /device:TPU:15, one launch (start us, length us, event | category | flops | bytes accessed | tf_op | source)
XLA Modules:
  0.0 113.1 jit_solution(10976708011912706805)
XLA Ops:
  0.6 106.4 %shard_map.93 = (bf16[512,1024]{1,0:T(8,128)(2,1)}, bf16[512,512]{1,0:T(8,128)(2,1)}, bf16[512,512]{1,0:T(8,128)(2,1)}, f32[320,1024]{1,0:T(8,128)}) custom-call(bf16[512,1024]{1,0:T(8,128)(2,1)} %q_hbm.1, bf16[512,512]{1,0:T(8,128)(2,1)} %k_hbm.1, bf16[512,512]{1,0:T(8,128)(2,1)} %v_hbm.1, s32[1,512]{1,0:T(1,128)} %bitcast.1, bf16[512,2560]{1,0:T(8,128)(2,1)} %cot_hbm.1, ...), custom_call_target="tpu_custom_call" | custom-call | tf_op jit(solution)/shard_map/pallas_call | solution.py:352
  107.0 0.0 copy-start.1
  107.0 0.0 copy-start
  107.0 2.4 %copy.14 = bf16[512,1024]{1,0:T(8,128)(2,1)} copy(bf16[512,1024]{1,0:T(8,128)(2,1)} %get-tuple-element.8) | data formatting | bytes 2097152
  109.4 1.9 %copy.15 = bf16[512,512]{1,0:T(8,128)(2,1)} copy(bf16[512,512]{1,0:T(8,128)(2,1)} %get-tuple-element.9) | data formatting | bytes 1048576
  111.3 0.0 copy-done.1
  111.3 0.8 copy.16
  112.1 0.0 copy-done
  112.1 1.1 copy.17
Async XLA Ops:
  107.0 4.3 %copy-start.1 = (bf16[512,512]{1,0:T(8,128)(2,1)S(1)}, bf16[512,512]{1,0:T(8,128)(2,1)}, u32[]{:S(2)}) copy-start(bf16[512,512]{1,0:T(8,128)(2,1)} %get-tuple-element.10) | copy-start | bytes 1572868
  107.0 5.1 %copy-start = (f32[320,1024]{1,0:T(8,128)S(1)}, f32[320,1024]{1,0:T(8,128)}, u32[]{:S(2)}) copy-start(f32[320,1024]{1,0:T(8,128)} %get-tuple-element.11) | copy-start | bytes 3932164

commit v2 on v1

--- a/solution.py
+++ b/solution.py
@@ -35,9 +35,9 @@
     dq_ref, dk_ref, dv_ref, gow_ref,
     q_s, w_s, cot_s, cot_t, da_s, at_s, kall, vall, seg_s, bias_s, prob_s, dk_acc, dv_acc,
     mid_send, mid_recv, back_send, back_recv,
-    own_part, pair_send, pair_recv, far_send, far_recv, own_sum,
+    own_part, pair_send, pair_recv, far_send, far_recv, relay_recv, direct_recv, own_sum,
     in_sem, halo_ss, halo_rs, fwd_ss, fwd_rs, mid_ss, mid_rs, back_ss, back_rs,
-    pair_ss, pair_rs, far_ss, far_rs,
+    pair_ss, pair_rs, far_ss, far_rs, relay_ss, relay_rs, direct_ss, direct_rs,
 ):
     heads = ng * groups
     rows = q_hbm.shape[0]
@@ -51,6 +51,10 @@
     below = lax.rem(z + nz - 1, nz)
     has_above = z < nz - 1
     has_below = z > 0
+    couple = z // 2
+    odd = lax.rem(z, 2)
+    partner = z + 1 - 2 * odd
+    pairs = nz // 2
 
     def cols(h):
         return pl.ds(h * DH, DH)
@@ -191,17 +195,30 @@
             device_id={"sub": peer}, device_id_type=MESH,
         )
 
-    def far_send_copy(h, d):
-        return pltpu.make_async_remote_copy(
-            src_ref=far_send.at[h, d], dst_ref=far_recv.at[h, z],
-            send_sem=far_ss.at[h, d], recv_sem=far_rs.at[h, z],
-            device_id={"ctx": d}, device_id_type=MESH,
-        )
-
-    def far_recv_copy(h, d):
-        return pltpu.make_async_remote_copy(
-            src_ref=far_send.at[h, d], dst_ref=far_recv.at[h, d],
-            send_sem=far_ss.at[h, d], recv_sem=far_rs.at[h, d],
+    def handed(d):
+        return ((odd == 0) & (d >= 2 * couple + 2)) | ((odd == 1) & (d < 2 * couple))
+
+    def taken(d):
+        return ((odd == 1) & (d >= 2 * couple + 2)) | ((odd == 0) & (d < 2 * couple))
+
+    def relay_copy(h, d):
+        return pltpu.make_async_remote_copy(
+            src_ref=far_send.at[h, d], dst_ref=relay_recv.at[h, d],
+            send_sem=relay_ss.at[h, d], recv_sem=relay_rs.at[h, d],
+            device_id={"ctx": partner}, device_id_type=MESH,
+        )
+
+    def direct_copy(h):
+        return pltpu.make_async_remote_copy(
+            src_ref=far_send.at[h, partner], dst_ref=direct_recv.at[h],
+            send_sem=direct_ss.at[h], recv_sem=direct_rs.at[h],
+            device_id={"ctx": partner}, device_id_type=MESH,
+        )
+
+    def far_copy(h, d, slot):
+        return pltpu.make_async_remote_copy(
+            src_ref=far_send.at[h, d], dst_ref=far_recv.at[h, slot],
+            send_sem=far_ss.at[h, d], recv_sem=far_rs.at[h, slot],
             device_id={"ctx": d}, device_id_type=MESH,
         )
 
@@ -220,6 +237,81 @@
 
             last = pl.ds(2 * rows, rows)
             acc[g, last] = acc[g, last] + jnp.where(s == 0, other, 0.0)
+
+    def attend(g, h):
+        slot = h % groups
+
+        def block(b, carry):
+            mine = pl.ds(pl.multiple_of(b * QB, QB), QB)
+            reach = pl.ds(pl.multiple_of(b * QB, QB), SPAN)
+            scores = dot_nt(q_s[h, mine], kall[g, reach]) * scale + bias_s[b]
+            top = jnp.max(scores, axis=1, keepdims=True)
+            raised = jnp.exp(scores - top)
+            probs = raised * (1.0 / jnp.sum(raised, axis=1, keepdims=True))
+            prob_s[slot, b] = probs
+            at_s[slot, mine] = dot_nn(probs.astype(BF16), vall[g, reach]).astype(BF16)
+            return carry
+
+        lax.fori_loop(0, rows // QB, block, 0)
+
+    def attend_back(g, h):
+        slot = h % groups
+
+        def block(b, carry):
+            mine = pl.ds(pl.multiple_of(b * QB, QB), QB)
+            reach = pl.ds(pl.multiple_of(b * QB, QB), SPAN)
+            grad = da_s[h, mine]
+            probs = prob_s[slot, b]
+            delta = jnp.sum(at_s[slot, mine].astype(F32) * grad.astype(F32), axis=1, keepdims=True)
+            dscores = (probs * (dot_nt(grad, vall[g, reach]) - delta)).astype(BF16)
+            dq_ref[mine, cols(h)] = (dot_nn(dscores, kall[g, reach]) * scale).astype(BF16)
+            dk_acc[g, reach] += dot_tn(dscores, q_s[h, mine])
+            dv_acc[g, reach] += dot_tn(probs.astype(BF16), grad)
+            return carry
+
+        lax.fori_loop(0, rows // QB, block, 0)
+
+    def weight_parts(h):
+        slot = h % groups
+
+        def peers(d, carry):
+            pair_send[h, d] = dot_nn(cot_t[part_rows(d, peer)], at_s[slot]).astype(BF16)
+            return carry
+
+        lax.fori_loop(0, nz, peers, 0)
+        pair_copy(h).start()
+
+        def owns(d, carry):
+            own_part[h % 2, d] = dot_nn(cot_t[part_rows(d, s)], at_s[slot])
+            return carry
+
+        lax.fori_loop(0, nz, owns, 0)
+
+    def weight_out(h):
+        pair_copy(h).wait_recv()
+
+        def both(d, carry):
+            far_send[h, d] = (own_part[h % 2, d] + pair_recv[h, d].astype(F32)).astype(BF16)
+            return carry
+
+        lax.fori_loop(0, nz, both, 0)
+        for d in range(nz):
+
+            @pl.when(handed(d))
+            def _():
+                relay_copy(h, d).start()
+
+        direct_copy(h).start()
+        own_sum[h] = own_part[h % 2, z] + pair_recv[h, z].astype(F32)
+
+    def weight_relay(h):
+        for d in range(nz):
+
+            @pl.when(taken(d))
+            def _():
+                relay_copy(h, d).wait_recv()
+                far_send[h, d] = (far_send[h, d].astype(F32) + relay_recv[h, d].astype(F32)).astype(BF16)
+                far_copy(h, d, couple).start()
 
     for g in range(ng):
         load_kv[g][0].wait()
@@ -227,76 +319,39 @@
         arrive([1 + 2 * g, 2 + 2 * g])
         dk_acc[g] = jnp.zeros((3 * rows, DH), F32)
         dv_acc[g] = jnp.zeros((3 * rows, DH), F32)
-        for h in range(g * groups, (g + 1) * groups):
+        here = range(g * groups, (g + 1) * groups)
+        for h in here:
             load_q[h].wait()
-
-            def attend(b, carry):
-                mine = pl.ds(pl.multiple_of(b * QB, QB), QB)
-                reach = pl.ds(pl.multiple_of(b * QB, QB), SPAN)
-                scores = dot_nt(q_s[h, mine], kall[g, reach]) * scale + bias_s[b]
-                top = jnp.max(scores, axis=1, keepdims=True)
-                raised = jnp.exp(scores - top)
-                probs = raised * (1.0 / jnp.sum(raised, axis=1, keepdims=True))
-                prob_s[b] = probs
-                at_s[mine] = dot_nn(probs.astype(BF16), vall[g, reach]).astype(BF16)
-                return carry
-
-            lax.fori_loop(0, rows // QB, attend, 0)
-
-            def weight_part(d, carry):
-                pair_send[h, d] = dot_nn(cot_t[part_rows(d, peer)], at_s[...]).astype(BF16)
-                return carry
-
-            lax.fori_loop(0, nz, weight_part, 0)
-            pair_copy(h).start()
-
-            def weight_own(d, carry):
-                own_part[d] = dot_nn(cot_t[part_rows(d, s)], at_s[...])
-                return carry
-
-            lax.fori_loop(0, nz, weight_own, 0)
-
-            def attend_back(b, carry):
-                mine = pl.ds(pl.multiple_of(b * QB, QB), QB)
-                reach = pl.ds(pl.multiple_of(b * QB, QB), SPAN)
-                grad = da_s[h, mine]
-                probs = prob_s[b]
-                delta = jnp.sum(at_s[mine].astype(F32) * grad.astype(F32), axis=1, keepdims=True)
-                dscores = (probs * (dot_nt(grad, vall[g, reach]) - delta)).astype(BF16)
-                dq_ref[mine, cols(h)] = (dot_nn(dscores, kall[g, reach]) * scale).astype(BF16)
-                dk_acc[g, reach] += dot_tn(dscores, q_s[h, mine])
-                dv_acc[g, reach] += dot_tn(probs.astype(BF16), grad)
-                return carry
-
-            lax.fori_loop(0, rows // QB, attend_back, 0)
-
-            pair_copy(h).wait_recv()
-
-            def pair_sum(d, carry):
-                total = own_part[d] + pair_recv[h, d].astype(F32)
-                own_part[d] = total
-                far_send[h, d] = total.astype(BF16)
-                return carry
-
-            lax.fori_loop(0, nz, pair_sum, 0)
-            own_sum[h] = own_part[z]
-            for step in range(1, nz):
-                far_send_copy(h, lax.rem(z + step, nz)).start()
-            if h == g * groups and g > 0:
-                send_back(g - 1)
-
+            attend(g, h)
+            if h > here[0]:
+                weight_out(h - 1)
+            weight_parts(h)
+            if g > 0:
+                if h == here[0]:
+                    send_back(g - 1)
+                weight_relay(h - groups)
+        for h in here:
+            attend_back(g, h)
+            if h == here[0]:
+                weight_out(here[-1])
         for j, acc in enumerate((dk_acc, dv_acc)):
             mid_send[g, j] = acc[g, middle].astype(BF16)
             mid_copy(g, j).start()
     send_back(ng - 1)
+    for h in range(heads - groups, heads):
+        weight_relay(h)
 
     for h in range(heads):
-        for step in range(1, nz):
-            far_recv_copy(h, lax.rem(z + step, nz)).wait_recv()
-        total = own_sum[h]
-        for step in range(1, nz):
-            total = total + far_recv[h, lax.rem(z + step, nz)].astype(F32)
-        gow_ref[:, cols(h)] = total * norm
+        direct_copy(h).wait_recv()
+        own_sum[h] = own_sum[h] + direct_recv[h].astype(F32)
+        for slot in range(pairs):
+
+            @pl.when(couple != slot)
+            def _():
+                far_copy(h, 0, slot).wait_recv()
+                own_sum[h] = own_sum[h] + far_recv[h, slot].astype(F32)
+
+        gow_ref[:, cols(h)] = own_sum[h] * norm
 
     last = pl.ds(2 * rows, rows)
 
@@ -334,8 +389,16 @@
 
     for h in range(heads):
         pair_copy(h).wait_send()
-        for step in range(1, nz):
-            far_send_copy(h, lax.rem(z + step, nz)).wait_send()
+        direct_copy(h).wait_send()
+        for d in range(nz):
+
+            @pl.when(handed(d))
+            def _():
+                relay_copy(h, d).wait_send()
+
+            @pl.when(taken(d))
+            def _():
+                far_copy(h, d, couple).wait_send()
 
 
 def shards(nz, queries, keys, values, segment, cotangent, out_weight):
@@ -365,17 +428,20 @@
             pltpu.VMEM((rows, width), BF16),
             pltpu.VMEM((width, rows), BF16),
             pltpu.VMEM((heads, rows, DH), BF16),
-            pltpu.VMEM((rows, DH), BF16),
+            pltpu.VMEM((groups, rows, DH), BF16),
             pltpu.VMEM((ng, 3 * rows, DH), BF16),
             pltpu.VMEM((ng, 3 * rows, DH), BF16),
             pltpu.VMEM((3, 1, rows), jnp.int32),
             pltpu.VMEM((rows // QB, QB, SPAN), F32),
-            pltpu.VMEM((rows // QB, QB, SPAN), F32),
+            pltpu.VMEM((groups, rows // QB, QB, SPAN), F32),
             pltpu.VMEM((ng, 3 * rows, DH), F32),
             pltpu.VMEM((ng, 3 * rows, DH), F32),
             kv_block, kv_block, kv_block, kv_block,
-            pltpu.VMEM((nz, part, DH), F32),
-            parts, parts, parts, parts,
+            pltpu.VMEM((2, nz, part, DH), F32),
+            parts, parts, parts,
+            pltpu.VMEM((heads, nz // 2, part, DH), BF16),
+            parts,
+            pltpu.VMEM((heads, part, DH), BF16),
             pltpu.VMEM((heads, part, DH), F32),
             dma((2 + 2 * heads + 2 * ng,)),
             dma((2 * ng + 1,)), dma((2 * ng + 1,)),
@@ -383,7 +449,9 @@
             dma((ng, 2)), dma((ng, 2)),
             dma((ng, 2)), dma((ng, 2)),
             dma((heads,)), dma((heads,)),
+            dma((heads, nz)), dma((heads, nz // 2)),
             dma((heads, nz)), dma((heads, nz)),
+            dma((heads,)), dma((heads,)),
         ],
         compiler_params=pltpu.CompilerParams(
             collective_id=0, has_side_effects=True, vmem_limit_bytes=60 * 1024 * 1024

time: 113 us -> 98.1 us (0.87)
  the two profiles are of different devices: /device:TPU:15 before, /device:TPU:22 now
where the time goes in v2:
time: 98.1 us; the launch traced here: 97.9 us
  Pallas kernels  91.1 us (93%)
  local copies, waits for them, and re-layouts  6.12 us (6%)
    pallas_call x1, Pallas kernels, shards(): pl.pallas_call(functools.partial(layer_kernel, nz, ng, groups, norm), out...  91.1 us
    unnamed x8, local copies, waits for them, and re-layouts  6.12 us

profile of v2, /device:TPU:22, one launch (start us, length us, event | category | flops | bytes accessed | tf_op | source)
XLA Modules:
  0.0 97.9 jit_solution(6079996659042766470)
XLA Ops:
  0.6 91.1 %shard_map.93 = (bf16[512,1024]{1,0:T(8,128)(2,1)}, bf16[512,512]{1,0:T(8,128)(2,1)}, bf16[512,512]{1,0:T(8,128)(2,1)}, f32[320,1024]{1,0:T(8,128)}) custom-call(bf16[512,1024]{1,0:T(8,128)(2,1)} %q_hbm.1, bf16[512,512]{1,0:T(8,128)(2,1)} %k_hbm.1, bf16[512,512]{1,0:T(8,128)(2,1)} %v_hbm.1, s32[1,512]{1,0:T(1,128)} %bitcast.1, bf16[512,2560]{1,0:T(8,128)(2,1)} %cot_hbm.1, ...), custom_call_target="tpu_custom_call" | custom-call | tf_op jit(solution)/shard_map/pallas_call | solution.py:415
  91.8 0.0 copy-start.1
  91.8 0.0 copy-start
  91.8 2.4 %copy.14 = bf16[512,1024]{1,0:T(8,128)(2,1)} copy(bf16[512,1024]{1,0:T(8,128)(2,1)} %get-tuple-element.8) | data formatting | bytes 2097152
  94.2 1.9 %copy.15 = bf16[512,512]{1,0:T(8,128)(2,1)} copy(bf16[512,512]{1,0:T(8,128)(2,1)} %get-tuple-element.9) | data formatting | bytes 1048576
  96.1 0.0 copy-done.1
  96.1 0.8 copy.16
  96.9 0.0 copy-done
  96.9 1.1 %copy.17 = f32[320,1024]{1,0:T(8,128)} copy(f32[320,1024]{1,0:T(8,128)S(1)} %copy-done) | data formatting | bytes 2621440
Async XLA Ops:
  91.8 4.3 %copy-start.1 = (bf16[512,512]{1,0:T(8,128)(2,1)S(1)}, bf16[512,512]{1,0:T(8,128)(2,1)}, u32[]{:S(2)}) copy-start(bf16[512,512]{1,0:T(8,128)(2,1)} %get-tuple-element.10) | copy-start | bytes 1572868
  91.8 5.1 %copy-start = (f32[320,1024]{1,0:T(8,128)S(1)}, f32[320,1024]{1,0:T(8,128)}, u32[]{:S(2)}) copy-start(f32[320,1024]{1,0:T(8,128)} %get-tuple-element.11) | copy-start | bytes 3932164

commit v3 on v2

--- a/solution.py
+++ b/solution.py
@@ -111,7 +111,7 @@
 
     @pl.when(has_above)
     def _():
-        for copy in halos:
+        for copy in halos[:3]:
             copy.start()
 
     @pl.when(s == 0)
@@ -161,6 +161,15 @@
 
     for j in range(width // DH):
         cot_t[pl.ds(j * DH, DH)] = cot_s[:, cols(j)].T
+
+    for g in range(1, ng):
+
+        @pl.when(has_above)
+        def _():
+            halos[2 * g - 1].wait_send()
+            halos[2 * g].wait_send()
+            halos[2 * g + 1].start()
+            halos[2 * g + 2].start()
 
     load_seg.wait()
     arrive([0])
@@ -301,7 +310,10 @@
             def _():
                 relay_copy(h, d).start()
 
-        direct_copy(h).start()
+        if h > 0:
+            direct_copy(h - 1).start()
+        if h == heads - 1:
+            direct_copy(h).start()
         own_sum[h] = own_part[h % 2, z] + pair_recv[h, z].astype(F32)
 
     def weight_relay(h):
@@ -371,7 +383,7 @@
 
     @pl.when(has_above)
     def _():
-        for copy in halos:
+        for copy in [halos[0]] + halos[2 * ng - 1 :]:
             copy.wait_send()
 
     @pl.when(has_below | (s == 0))
@@ -399,6 +411,11 @@
             @pl.when(taken(d))
             def _():
                 far_copy(h, d, couple).wait_send()
+
+
+def store_kernel(*refs):
+    for src, dst in zip(refs[:4], refs[4:]):
+        dst[...] = src[...]
 
 
 def shards(nz, queries, keys, values, segment, cotangent, out_weight):
@@ -412,14 +429,15 @@
     kv_block = pltpu.VMEM((ng, 2, rows, DH), BF16)
     parts = pltpu.VMEM((heads, nz, part, DH), BF16)
     dma = pltpu.SemaphoreType.DMA
-    return pl.pallas_call(
+    shapes = (
+        jax.ShapeDtypeStruct(queries.shape, BF16),
+        jax.ShapeDtypeStruct(keys.shape, BF16),
+        jax.ShapeDtypeStruct(values.shape, BF16),
+        jax.ShapeDtypeStruct((part, heads * DH), F32),
+    )
+    grads = pl.pallas_call(
         functools.partial(layer_kernel, nz, ng, groups, norm),
-        out_shape=(
-            jax.ShapeDtypeStruct(queries.shape, BF16),
-            jax.ShapeDtypeStruct(keys.shape, BF16),
-            jax.ShapeDtypeStruct(values.shape, BF16),
-            jax.ShapeDtypeStruct((part, heads * DH), F32),
-        ),
+        out_shape=shapes,
         in_specs=[pl.BlockSpec(memory_space=pl.ANY)] * 6,
         out_specs=[pl.BlockSpec(memory_space=pltpu.VMEM)] * 4,
         scratch_shapes=[
@@ -457,6 +475,10 @@
             collective_id=0, has_side_effects=True, vmem_limit_bytes=60 * 1024 * 1024
         ),
     )(queries, keys, values, segment.reshape(1, rows), cotangent, out_weight)
+    halves = [pl.BlockSpec((a.shape[0] // 2, a.shape[1]), lambda i: (i, 0)) for a in shapes]
+    return pl.pallas_call(
+        store_kernel, grid=(2,), out_shape=shapes, in_specs=halves, out_specs=halves,
+    )(*grads)
 
 
 def solution(mesh):

time: 98.1 us -> 94.5 us (0.963)
  local copies, waits for them, and re-layouts: 6.12 us -> 0 us
  Pallas kernels: 91.1 us -> 93.7 us
    unnamed x8 -> x0, local copies, waits for them, and re-layouts: 6.12 us -> none
    pallas_call x0 -> x1, Pallas kernels: none -> 3.28 us  [shards(): pl.pallas_call(store_kernel, grid=(2,), out_shape=shapes, in_specs=halves...]
where the time goes in v3:
time: 94.5 us; the launch traced here: 94.3 us
  Pallas kernels  93.7 us (99%)
    pallas_call x1, Pallas kernels, shards(): pl.pallas_call(functools.partial(layer_kernel, nz, ng, groups, norm), out...  90.4 us
    pallas_call x1, Pallas kernels, shards(): pl.pallas_call(store_kernel, grid=(2,), out_shape=shapes, in_specs=halves...  3.28 us

profile of v3, /device:TPU:22, one launch (start us, length us, event | category | flops | bytes accessed | tf_op | source)
XLA Modules:
  0.0 94.3 jit_solution(4660892034415431329)
XLA Ops:
  0.6 90.4 %shard_map.93 = (bf16[512,1024]{1,0:T(8,128)(2,1)}, bf16[512,512]{1,0:T(8,128)(2,1)}, bf16[512,512]{1,0:T(8,128)(2,1)}, f32[320,1024]{1,0:T(8,128)}) custom-call(bf16[512,1024]{1,0:T(8,128)(2,1)} %q_hbm.1, bf16[512,512]{1,0:T(8,128)(2,1)} %k_hbm.1, bf16[512,512]{1,0:T(8,128)(2,1)} %v_hbm.1, s32[1,512]{1,0:T(1,128)} %bitcast.1, bf16[512,2560]{1,0:T(8,128)(2,1)} %cot_hbm.1, ...), custom_call_target="tpu_custom_call" | custom-call | tf_op jit(solution)/shard_map/pallas_call | solution.py:438
  91.1 3.3 %shard_map.94 = (bf16[512,1024]{1,0:T(8,128)(2,1)}, bf16[512,512]{1,0:T(8,128)(2,1)}, bf16[512,512]{1,0:T(8,128)(2,1)}, f32[320,1024]{1,0:T(8,128)}) custom-call(bf16[512,1024]{1,0:T(8,128)(2,1)} %get-tuple-element.8.refs_0_, bf16[512,512]{1,0:T(8,128)(2,1)} %get-tuple-element.9.refs_1_, bf16[512,512]{1,0:T(8,128)(2,1)} %get-tuple-element.10.refs_2_, ...), custom_call_target="tpu_custom_call" | custom-call | tf_op jit(solution)/shard_map/pallas_call | solution.py:479
